TPU v7x, 32 devices: a whole 2x2x4 slice. The times are simulated.
32 devices in a mesh: dp: 4 (over x, core), fsdp: 8 (over z, y).
Axes of the slice: x: 2, y: 2, z: 4, core: 2. Of those that a mesh axis runs over, the one named last changes fastest.
Arguments:
- tokens: bfloat16 [18432, 576], P(('dp', 'fsdp')), may hold values from -6 to 6
- cotangent: bfloat16 [18432, 576], P(('dp', 'fsdp')), may hold values from -6 to 6
- w_query: bfloat16 [576, 576], P(None, 'fsdp'), may hold values from -0.25 to 0.25
- key_projection_weight: bfloat16 [576, 192], P(None, 'fsdp'), may hold values from -0.25 to 0.25
- value_projection_weight: bfloat16 [576, 192], P(None, 'fsdp'), may hold values from -0.25 to 0.25
- output_projection_weight: bfloat16 [576, 576], P(None, 'fsdp'), may hold values from -0.75 to 0.75
- w_gate: bfloat16 [576, 1536], P(None, 'fsdp'), may hold values from -0.25 to 0.25
- w_up: bfloat16 [576, 1536], P(None, 'fsdp'), may hold values from -0.25 to 0.25
- w_down: bfloat16 [1536, 576], P(None, 'fsdp'), may hold values from -0.21875 to 0.21875
- gain_attn: bfloat16 [576], P('fsdp'), may hold values from 0.099609375 to 1.8984375
- gain_mlp: bfloat16 [576], P('fsdp'), may hold values from 0.099609375 to 1.8984375
Outputs:
- output: bfloat16 [18432, 576], P(('dp', 'fsdp'))
- grad_tokens: bfloat16 [18432, 576], P(('dp', 'fsdp'))
- grad_query: float32 [576, 576], P(None, 'fsdp')
- grad_key: float32 [576, 192], P(None, 'fsdp')
- grad_value: float32 [576, 192], P(None, 'fsdp')
- grad_out: float32 [576, 576], P(None, 'fsdp')
- grad_gate: float32 [576, 1536], P(None, 'fsdp')
- grad_up: float32 [576, 1536], P(None, 'fsdp')
- grad_down: float32 [1536, 576], P(None, 'fsdp')
- grad_gain_attn: float32 [576], P('fsdp')
- grad_gain_mlp: float32 [576], P('fsdp')
All inputs are finite; a program needn't handle non-finite values.
Results may differ from a plain program's by a relative error of at most 0.017.
Values may be sent and summed in bfloat16 or wider, within the bound.
No kernel may reach another device: no remote copies, remote signals or barrier semaphores. Data moves between devices by JAX's collectives and lax.ppermute only.
A program may use at most 128 MiB of HBM per device.

v0:
```python
import jax
import jax.numpy as jnp
from jax import lax
from jax.sharding import PartitionSpec as P

QUERY_HEADS = 9
KEY_VALUE_HEADS = 3
HEAD_SIZE = 64
SEQUENCE_LENGTH = 192
EPS_NORM = 1e-05
ROPE_BASE = 100000.0


def matrix_product(left, right):
    return jnp.dot(left, right, preferred_element_type=jnp.float32)


def einsum_mixed(form, left, right):
    return jnp.einsum(form, left, right, preferred_element_type=jnp.float32)


def rope_tables(length, head):
    half = head // 2
    position = jnp.arange(length).astype(jnp.float32)
    freqs = ROPE_BASE ** (-(jnp.arange(half).astype(jnp.float32) * 2.0 / head))
    angles = position[:, None] * freqs[None, :]
    return (jnp.cos(angles)[:, None, :], jnp.sin(angles)[:, None, :])


def apply_rotary_embedding(value_rows, cosine_table, sine_table):
    half = value_rows.shape[-1] // 2
    first = value_rows[..., :half]
    second = value_rows[..., half:]
    return jnp.concatenate(
        [first * cosine_table - second * sine_table, second * cosine_table + first * sine_table], -1
    )


def reverse_rotary_embedding(value_rows, cosine_table, sine_table):
    half = value_rows.shape[-1] // 2
    first = value_rows[..., :half]
    second = value_rows[..., half:]
    return jnp.concatenate(
        [first * cosine_table + second * sine_table, second * cosine_table - first * sine_table], -1
    )


def causal_mask():
    places = jnp.arange(SEQUENCE_LENGTH)
    return places[:, None] >= places[None, :]


def layer_forward(tokens, weights, cosine_table, sine_table):
    (
        w_query,
        key_projection_weight,
        value_projection_weight,
        output_projection_weight,
        w_gate,
        w_up,
        w_down,
        gain_attn,
        gain_mlp,
    ) = weights
    token_rows = tokens.shape[0]
    sequence_count = token_rows // SEQUENCE_LENGTH
    query_group_size = QUERY_HEADS // KEY_VALUE_HEADS
    allowed = causal_mask()
    xfull = tokens.astype(jnp.float32)
    inv_one = lax.rsqrt(jnp.mean(xfull * xfull, -1, keepdims=True) + EPS_NORM)
    first_normed_input = (xfull * inv_one * gain_attn.astype(jnp.float32)).astype(jnp.bfloat16)
    query_rows = apply_rotary_embedding(
        matrix_product(first_normed_input, w_query).reshape(
            sequence_count, SEQUENCE_LENGTH, QUERY_HEADS, HEAD_SIZE
        ),
        cosine_table,
        sine_table,
    ).astype(jnp.bfloat16)
    key_rows = apply_rotary_embedding(
        matrix_product(first_normed_input, key_projection_weight).reshape(
            sequence_count, SEQUENCE_LENGTH, KEY_VALUE_HEADS, HEAD_SIZE
        ),
        cosine_table,
        sine_table,
    ).astype(jnp.bfloat16)
    value_rows = (
        matrix_product(first_normed_input, value_projection_weight)
        .reshape(sequence_count, SEQUENCE_LENGTH, KEY_VALUE_HEADS, HEAD_SIZE)
        .astype(jnp.bfloat16)
    )
    grouped_queries = query_rows.reshape(
        sequence_count, SEQUENCE_LENGTH, KEY_VALUE_HEADS, query_group_size, HEAD_SIZE
    )
    scores = einsum_mixed("nqkgd,nskd->nkgqs", grouped_queries, key_rows) * HEAD_SIZE ** (-0.5)
    expo = jnp.where(allowed, jnp.exp(jnp.where(allowed, scores, 0.0)), 0.0)
    log_total = jnp.log(jnp.sum(expo, -1, keepdims=True))
    probs = jnp.where(allowed, jnp.exp(scores - log_total), 0.0).astype(jnp.bfloat16)
    attention_output = (
        einsum_mixed("nkgqs,nskd->nqkgd", probs, value_rows)
        .reshape(token_rows, QUERY_HEADS * HEAD_SIZE)
        .astype(jnp.bfloat16)
    )
    middle = xfull + matrix_product(attention_output, output_projection_weight)
    inv_two = lax.rsqrt(jnp.mean(middle * middle, -1, keepdims=True) + EPS_NORM)
    normed_two = (middle * inv_two * gain_mlp.astype(jnp.float32)).astype(jnp.bfloat16)
    gate = matrix_product(normed_two, w_gate)
    upper = matrix_product(normed_two, w_up)
    hidden = (jax.nn.silu(gate) * upper).astype(jnp.bfloat16)
    output = (middle + matrix_product(hidden, w_down)).astype(jnp.bfloat16)
    saved = (
        xfull,
        inv_one,
        first_normed_input,
        grouped_queries,
        key_rows,
        value_rows,
        log_total,
        attention_output,
        middle,
        inv_two,
        normed_two,
        gate,
        upper,
        hidden,
    )
    return (output, saved)


def keep_local(gradients):
    return gradients


def layer_backward(cotangent, saved, weights, cosine_table, sine_table, mlp_handler):
    (
        w_query,
        key_projection_weight,
        value_projection_weight,
        output_projection_weight,
        w_gate,
        w_up,
        w_down,
        gain_attn,
        gain_mlp,
    ) = weights
    (
        xfull,
        inv_one,
        first_normed_input,
        grouped_queries,
        key_rows,
        value_rows,
        log_total,
        attention_output,
        middle,
        inv_two,
        normed_two,
        gate,
        upper,
        hidden,
    ) = saved
    token_rows = cotangent.shape[0]
    sequence_count = token_rows // SEQUENCE_LENGTH
    query_group_size = QUERY_HEADS // KEY_VALUE_HEADS
    allowed = causal_mask()
    grad_down = matrix_product(hidden.T, cotangent)
    dhidden = matrix_product(cotangent, w_down.T)
    sigma = jax.nn.sigmoid(gate)
    dgate = (dhidden * upper * sigma * (1.0 + gate * (1.0 - sigma))).astype(jnp.bfloat16)
    dupper = (dhidden * gate * sigma).astype(jnp.bfloat16)
    grad_gate = matrix_product(normed_two.T, dgate)
    grad_up = matrix_product(normed_two.T, dupper)
    dnormed_two = matrix_product(dgate, w_gate.T) + matrix_product(dupper, w_up.T)
    unit_two = middle * inv_two
    grad_gain_mlp = jnp.sum(dnormed_two * unit_two, 0)
    mlp_result = mlp_handler((grad_gate, grad_up, grad_down, grad_gain_mlp))
    scaled_two = dnormed_two * gain_mlp.astype(jnp.float32)
    dmiddle = inv_two * (
        scaled_two - unit_two * jnp.mean(scaled_two * unit_two, -1, keepdims=True)
    ) + cotangent.astype(jnp.float32)
    middle_gradient_block = dmiddle.astype(jnp.bfloat16)
    grad_out = matrix_product(attention_output.T, middle_gradient_block)
    attention_gradient = (
        matrix_product(middle_gradient_block, output_projection_weight.T)
        .astype(jnp.bfloat16)
        .reshape(sequence_count, SEQUENCE_LENGTH, KEY_VALUE_HEADS, query_group_size, HEAD_SIZE)
    )
    scores = einsum_mixed("nqkgd,nskd->nkgqs", grouped_queries, key_rows) * HEAD_SIZE ** (-0.5)
    probs = jnp.where(allowed, jnp.exp(scores - log_total), 0.0).astype(jnp.bfloat16)
    softmax_correction = jnp.sum(
        attention_gradient.astype(jnp.float32)
        * attention_output.reshape(
            sequence_count, SEQUENCE_LENGTH, KEY_VALUE_HEADS, query_group_size, HEAD_SIZE
        ).astype(jnp.float32),
        -1,
    )
    softmax_correction = jnp.transpose(softmax_correction, (0, 2, 3, 1))[..., None]
    value_gradient_rows = einsum_mixed("nkgqs,nqkgd->nskd", probs, attention_gradient)
    dprobs = einsum_mixed("nqkgd,nskd->nkgqs", attention_gradient, value_rows)
    dscores = (
        probs.astype(jnp.float32) * (dprobs - softmax_correction) * HEAD_SIZE ** (-0.5)
    ).astype(jnp.bfloat16)
    dqueries = einsum_mixed("nkgqs,nskd->nqkgd", dscores, key_rows).reshape(
        sequence_count, SEQUENCE_LENGTH, QUERY_HEADS, HEAD_SIZE
    )
    key_gradient_rows = einsum_mixed("nkgqs,nqkgd->nskd", dscores, grouped_queries)
    dq_flat = (
        reverse_rotary_embedding(dqueries, cosine_table, sine_table)
        .reshape(token_rows, QUERY_HEADS * HEAD_SIZE)
        .astype(jnp.bfloat16)
    )
    key_gradient_flat = (
        reverse_rotary_embedding(key_gradient_rows, cosine_table, sine_table)
        .reshape(token_rows, KEY_VALUE_HEADS * HEAD_SIZE)
        .astype(jnp.bfloat16)
    )
    value_gradient_flat = value_gradient_rows.reshape(
        token_rows, KEY_VALUE_HEADS * HEAD_SIZE
    ).astype(jnp.bfloat16)
    grad_query = matrix_product(first_normed_input.T, dq_flat)
    grad_key = matrix_product(first_normed_input.T, key_gradient_flat)
    grad_value = matrix_product(first_normed_input.T, value_gradient_flat)
    dnormed_one = (
        matrix_product(dq_flat, w_query.T)
        + matrix_product(key_gradient_flat, key_projection_weight.T)
        + matrix_product(value_gradient_flat, value_projection_weight.T)
    )
    unit_one = xfull * inv_one
    grad_gain_attn = jnp.sum(dnormed_one * unit_one, 0)
    scaled_one = dnormed_one * gain_attn.astype(jnp.float32)
    grad_tokens = (
        inv_one * (scaled_one - unit_one * jnp.mean(scaled_one * unit_one, -1, keepdims=True))
        + dmiddle
    ).astype(jnp.bfloat16)
    attn_result = (grad_query, grad_key, grad_value, grad_out, grad_gain_attn)
    return (grad_tokens, attn_result, mlp_result)


def body(
    tokens,
    cotangent,
    w_query,
    key_projection_weight,
    value_projection_weight,
    output_projection_weight,
    w_gate,
    w_up,
    w_down,
    gain_attn,
    gain_mlp,
):
    cosine_table, sine_table = rope_tables(SEQUENCE_LENGTH, HEAD_SIZE)
    gathered = (
        lax.all_gather(w_query, "fsdp", axis=1, tiled=True),
        lax.all_gather(key_projection_weight, "fsdp", axis=1, tiled=True),
        lax.all_gather(value_projection_weight, "fsdp", axis=1, tiled=True),
        lax.all_gather(output_projection_weight, "fsdp", axis=1, tiled=True),
        lax.all_gather(w_gate, "fsdp", axis=1, tiled=True),
        lax.all_gather(w_up, "fsdp", axis=1, tiled=True),
        lax.all_gather(w_down, "fsdp", axis=1, tiled=True),
        lax.all_gather(gain_attn, "fsdp", axis=0, tiled=True),
        lax.all_gather(gain_mlp, "fsdp", axis=0, tiled=True),
    )
    output, saved = layer_forward(tokens, gathered, cosine_table, sine_table)
    grad_tokens, attn_part, mlp_part = layer_backward(
        cotangent, saved, gathered, cosine_table, sine_table, keep_local
    )
    shares = (
        lax.psum_scatter(attn_part[0], "fsdp", scatter_dimension=1, tiled=True),
        lax.psum_scatter(attn_part[1], "fsdp", scatter_dimension=1, tiled=True),
        lax.psum_scatter(attn_part[2], "fsdp", scatter_dimension=1, tiled=True),
        lax.psum_scatter(attn_part[3], "fsdp", scatter_dimension=1, tiled=True),
        lax.psum_scatter(mlp_part[0], "fsdp", scatter_dimension=1, tiled=True),
        lax.psum_scatter(mlp_part[1], "fsdp", scatter_dimension=1, tiled=True),
        lax.psum_scatter(mlp_part[2], "fsdp", scatter_dimension=1, tiled=True),
        lax.psum_scatter(attn_part[4], "fsdp", scatter_dimension=0, tiled=True),
        lax.psum_scatter(mlp_part[3], "fsdp", scatter_dimension=0, tiled=True),
    )
    summed = (
        lax.psum(shares[0].astype(jnp.bfloat16), "dp").astype(jnp.float32),
        lax.psum(shares[1].astype(jnp.bfloat16), "dp").astype(jnp.float32),
        lax.psum(shares[2].astype(jnp.bfloat16), "dp").astype(jnp.float32),
        lax.psum(shares[3].astype(jnp.bfloat16), "dp").astype(jnp.float32),
        lax.psum(shares[4].astype(jnp.bfloat16), "dp").astype(jnp.float32),
        lax.psum(shares[5].astype(jnp.bfloat16), "dp").astype(jnp.float32),
        lax.psum(shares[6].astype(jnp.bfloat16), "dp").astype(jnp.float32),
        lax.psum(shares[7].astype(jnp.bfloat16), "dp").astype(jnp.float32),
        lax.psum(shares[8].astype(jnp.bfloat16), "dp").astype(jnp.float32),
    )
    return (
        output,
        grad_tokens,
        summed[0],
        summed[1],
        summed[2],
        summed[3],
        summed[4],
        summed[5],
        summed[6],
        summed[7],
        summed[8],
    )


def solution(mesh):
    in_specs = (
        P(("dp", "fsdp"), None),
        P(("dp", "fsdp"), None),
        P(None, "fsdp"),
        P(None, "fsdp"),
        P(None, "fsdp"),
        P(None, "fsdp"),
        P(None, "fsdp"),
        P(None, "fsdp"),
        P(None, "fsdp"),
        P("fsdp"),
        P("fsdp"),
    )
    out_specs = (
        P(("dp", "fsdp"), None),
        P(("dp", "fsdp"), None),
        P(None, "fsdp"),
        P(None, "fsdp"),
        P(None, "fsdp"),
        P(None, "fsdp"),
        P(None, "fsdp"),
        P(None, "fsdp"),
        P(None, "fsdp"),
        P("fsdp"),
        P("fsdp"),
    )
    return jax.shard_map(body, mesh=mesh, in_specs=in_specs, out_specs=out_specs, check_vma=False)
```

profile of v0, /device:TPU:0, one launch (start us, length us, event | category | flops | bytes accessed | tf_op | source)
XLA Modules:
  0.0 783.0 jit_solution(9801068825600758200)
XLA Ops:
  10.6 1.5 copy.76
  14.0 24.2 %all-reduce.9 = (bf16[576]{0:T(1024)(128)(2,1)S(1)}, bf16[576]{0:T(1024)(128)(2,1)}) all-reduce(bf16[576]{0:T(1024)(128)(2,1)S(1)} %dynamic-update-slice, bf16[576]{0:T(1024)(128)(2,1)S(1)} %dynamic-update-slice.1), channel_id=1, replica_groups=mesh['dp'=4,'fsdp'=8] {'fsdp'}, use_global_device_ids=true, to_apply=%add | all-reduce | flops 1152 | bytes 4608
  38.2 31.8 %all_gather.29 = bf16[576,192]{0,1:T(8,128)(2,1)S(1)} all-gather(bf16[576,24]{0,1:T(8,128)(2,1)S(1)} %copy-done.36), channel_id=1, replica_groups=mesh['dp'=4,'fsdp'=8] {'fsdp'}, dimensions={1}, use_global_device_ids=true | all-gather | bytes 248832 | tf_op jit(solution)/shard_map/all_gather | solution.py:254
  72.4 33.6 %all_gather.30 = bf16[576,576]{0,1:T(8,128)(2,1)S(1)} all-gather(bf16[576,72]{0,1:T(8,128)(2,1)S(1)} %copy-done.28), channel_id=1, replica_groups=mesh['dp'=4,'fsdp'=8] {'fsdp'}, dimensions={1}, use_global_device_ids=true | all-gather | bytes 746496 | tf_op jit(solution)/shard_map/all_gather | solution.py:253
  106.9 2.0 fusion.56
  108.9 2.8 reshape.146
  111.8 31.4 %all_gather.28 = bf16[576,192]{0,1:T(8,128)(2,1)S(1)} all-gather(bf16[576,24]{0,1:T(8,128)(2,1)S(1)} %copy-done.37), channel_id=1, replica_groups=mesh['dp'=4,'fsdp'=8] {'fsdp'}, dimensions={1}, use_global_device_ids=true | all-gather | bytes 248832 | tf_op jit(solution)/shard_map/all_gather | solution.py:255
  143.1 1.2 convolution_convert_fusion.2
  146.8 0.9 fusion.35
  147.7 2.8 fusion.3
  151.2 0.9 copy-done
  152.9 1.7 convert_element_type.233
  154.6 2.3 copy.88
  156.8 32.6 %all_gather.31 = bf16[576,576]{0,1:T(8,128)(2,1)S(1)} all-gather(bf16[576,72]{0,1:T(8,128)(2,1)S(1)} %copy-done.29), channel_id=1, replica_groups=mesh['dp'=4,'fsdp'=8] {'fsdp'}, dimensions={1}, use_global_device_ids=true | all-gather | bytes 746496 | tf_op jit(solution)/shard_map/all_gather | solution.py:256
  189.4 2.2 multiply_reduce_fusion.3
  191.6 1.2 multiply_convert_fusion.3
  192.9 5.2 fusion.61
  198.0 5.2 fusion.62
  203.2 7.9 %multiply_convert_fusion = (bf16[576,1536]{1,0:T(8,128)(2,1)S(1)}, bf16[576,1536]{1,0:T(8,128)(2,1)S(1)}, bf16[576,1536]{1,0:T(8,128)(2,1)}) fusion(f32[576,1536]{1,0:T(8,128)} %fusion.61, f32[576,1536]{1,0:T(8,128)} %fusion.62, bf16[576,576]{1,0:T(8,128)(2,1)} %param.12, bf16[1536,576]{0,1:T(8,128)(2,1)} %all-gather.8.cloned.1.call-done), kind=kOutput, calls=%fused_computation.13 | convolution fusion | flops 1033371648 | bytes 14819328 | tf_op jit(solution)/shard_map/dot_general | solution.py:15
  211.1 1.7 fusion.63
  212.9 1.0 copy-done.43
  213.9 1.9 multiply_reduce_fusion.1
  215.9 1.8 convert_add_fusion.1
  217.7 2.0 fusion.36
  219.9 2.8 convolution_convert_fusion.1
  222.8 3.9 reshape.170
  226.7 2.7 copy.91
  230.7 3.1 fusion.6
  234.6 1.5 fusion.31
  236.1 1.9 pad_maximum_fusion
  237.9 3.5 convert_element_type.247
  241.5 3.2 fusion.51
  244.7 5.6 fusion.66
  250.4 5.6 fusion.67
  256.2 5.1 fusion.68
  262.0 2.1 convolution_bitcast_fusion.1
  264.3 1.0 copy.97
  265.3 2.1 convert_element_type.248
  267.4 2.2 fusion.49
  269.7 2.1 fusion.34
  272.5 1.3 fusion.47
  273.8 1.7 fusion.64
  275.4 1.6 fusion.65
  277.1 4.4 fusion.26
  281.5 17.5 %all-reduce.8 = (bf16[576]{0:T(1024)(128)(2,1)S(1)}, bf16[576]{0:T(1024)(128)(2,1)S(1)}) all-reduce(f32[576]{0:T(1024)S(1)} %get-tuple-element.46, f32[576]{0:T(1024)S(1)} %get-tuple-element.44), channel_id=9, replica_groups=mesh['dp'=4,'fsdp'=8] {'fsdp'}, use_global_device_ids=true, to_apply=%region_21.22.clone | all-reduce | flops 1152 | bytes 6912
  299.1 1.8 fusion.25
  300.9 1.2 copy.105
  302.1 1.6 convert_element_type.259
  303.6 44.2 %reduce-scatter.22.cloned.1.call-done = f32[576,72]{0,1:T(8,128)} async-done(((f32[576,576]{0,1:T(8,128)}), f32[576,72]{0,1:T(8,128)}) %reduce-scatter.22.cloned.1.call-update) | async-done | bytes 165904
  347.8 1.6 convert_element_type.253
  349.4 85.5 %reduce-scatter.16.cloned.1.call-done = f32[576,192]{0,1:T(8,128)} async-done(((f32[576,1536]{0,1:T(8,128)}), f32[576,192]{0,1:T(8,128)}) %reduce-scatter.16.cloned.1.call-update) | async-done | bytes 442384 | tf_op jit(solution)/shard_map/reduce_scatter | solution.py:272
  434.9 1.8 convert_element_type.261
  436.7 86.2 %reduce-scatter.18.cloned.1.call-done = f32[576,192]{0,1:T(8,128)} async-done(((f32[576,1536]{0,1:T(8,128)}), f32[576,192]{0,1:T(8,128)}) %reduce-scatter.18.cloned.1.call-update) | async-done | bytes 442384 | tf_op jit(solution)/shard_map/reduce_scatter | solution.py:273
  522.8 1.7 convert_element_type.263
  524.6 81.0 %reduce-scatter.20.cloned.1.call-done = f32[1536,72]{0,1:T(8,128)} async-done(((f32[1536,576]{0,1:T(8,128)}), f32[1536,72]{0,1:T(8,128)}) %reduce-scatter.20.cloned.1.call-update) | async-done | bytes 442384 | tf_op jit(solution)/shard_map/reduce_scatter | solution.py:274
  605.6 1.7 convert_element_type.265
  607.3 3.6 add_convert_fusion
  610.9 1.2 copy.104
  612.1 57.2 %reduce-scatter.24.cloned.1.call-done = f32[576,24]{0,1:T(8,128)} async-done(((f32[576,192]{0,1:T(8,128)}), f32[576,24]{0,1:T(8,128)}) %reduce-scatter.24.cloned.1.call-update) | async-done | bytes 55312
  670.1 62.0 %reduce-scatter.26.cloned.1.call-done = f32[576,24]{0,1:T(8,128)} async-done(((f32[576,192]{0,1:T(8,128)}), f32[576,24]{0,1:T(8,128)}) %reduce-scatter.26.cloned.1.call-update) | async-done | bytes 55312
  732.9 10.9 %all-reduce.10 = (bf16[576,24]{0,1:T(8,128)(2,1)S(1)}, bf16[576,24]{0,1:T(8,128)(2,1)S(1)}, bf16[72]{0:T(256)(128)(2,1)S(1)}, bf16[72]{0:T(256)(128)(2,1)S(1)}) all-reduce(bf16[576,24]{0,1:T(8,128)(2,1)S(1)} %convert_element_type.255, bf16[576,24]{0,1:T(8,128)(2,1)S(1)} %convert_element_type.257, ...), channel_id=1, replica_groups=mesh['dp'=4,'fsdp'=8] {'dp'}, use_global_device_ids=true, to_apply=%region_9.10 | all-reduce | flops 27792 | bytes 111168 | tf_op jit(solution)/shard_map/psum | solution.py:280
  746.1 24.4 %all-reduce.14.cloned.1.call-done = (bf16[576,72]{0,1:T(8,128)(2,1)}, bf16[576,72]{0,1:T(8,128)(2,1)}, bf16[576,192]{0,1:T(8,128)(2,1)}, bf16[576,192]{0,1:T(8,128)(2,1)}, bf16[1536,72]{0,1:T(8,128)(2,1)}) async-done(((bf16[576,72]{0,1:T(8,128)(2,1)}, bf16[576,72]{0,1:T(8,128)(2,1)}, bf16[576,192]{0,1:T(8,128)(2,1)}, bf16[576,192]{0,1:T(8,128)(2,1)}, bf16[1536,72]{0,1:T(8,128)(2,1)}), ...) | async-done | bytes 829456 | tf_op jit(solution)/shard_map/psum | solution.py:279
  770.5 1.8 convert_element_type.262
  772.3 1.8 convert_element_type.264
  (164 shorter events, 21.6 us)
Async XLA Ops:
  7.2 5.1 copy-start.39
  7.2 6.3 copy-start.44
  7.2 6.6 copy-start.45
  7.2 31.0 %copy-start.36 = (bf16[576,24]{0,1:T(8,128)(2,1)S(1)}, bf16[576,24]{0,1:T(8,128)(2,1)}, u32[]{:S(2)}) copy-start(bf16[576,24]{0,1:T(8,128)(2,1)} %param.14) | copy-start | bytes 82948
  7.2 185.6 %all-gather.4.cloned.1.call-start = ((), (), s32[]{:S(2)}) async-start(), calls=%async_computation.7 | async-start | bytes 2211840 | tf_op jit(solution)/shard_map/all_gather | solution.py:257
  8.0 190.1 %all-gather.6.cloned.1.call-start = ((), (), s32[]{:S(2)}) async-start(), calls=%async_computation.8 | async-start | bytes 2211840 | tf_op jit(solution)/shard_map/all_gather | solution.py:258
  8.7 194.5 %all-gather.8.cloned.1.call-start = ((), (), s32[]{:S(2)}) async-start(), calls=%async_computation.9 | async-start | bytes 1990656 | tf_op jit(solution)/shard_map/all_gather | solution.py:259
  9.4 292.6 %reduce-scatter.28.cloned.1.call-start = ((), (), s32[]{:S(2)}) async-start(), calls=%async_computation.16 | async-start | bytes 1658880
  12.2 130.9 %copy-start.32 = (f32[576]{0:T(1024)}, f32[576]{0:T(1024)S(1)}, u32[]{:S(2)}) copy-start(f32[576]{0:T(1024)S(1)} %add_rsqrt_fusion.1) | copy-start | bytes 6916
  38.2 104.9 %copy-start.34 = (f32[576]{0:T(1024)}, f32[576]{0:T(1024)S(1)}, u32[]{:S(2)}) copy-start(f32[576]{0:T(1024)S(1)} %convert_element_type.224) | copy-start | bytes 6916
  70.0 0.7 copy-start.21
  71.1 1.2 copy-start.28
  106.0 0.9 copy-start.11
  108.9 2.9 copy-start.37
  111.7 32.5 %copy-start.40 = (f32[192]{0:T(256)S(1)}, f32[192]{0:T(256)}, u32[]{:S(2)}) copy-start(f32[192]{0:T(256)} %iota_convert_fusion) | copy-start | bytes 2308
  111.7 32.5 %copy-start.41 = (f32[32]{0:T(128)S(1)}, f32[32]{0:T(128)}, u32[]{:S(2)}) copy-start(f32[32]{0:T(128)} %negate_power_fusion) | copy-start | bytes 388
  143.1 1.4 copy-start.23
  144.5 1.0 copy-start.16
  145.5 1.1 copy-start.26
  145.6 2.1 copy-start.17
  145.6 2.1 copy-start.19
  145.7 2.0 copy-start.9
  146.6 1.1 copy-start.10
  146.8 3.8 copy-start.14
  150.5 1.6 copy-start
  152.9 1.7 copy-start.38
  152.9 4.0 copy-start.29
  189.4 2.2 copy-start.8
  191.6 21.2 %copy-start.5 = (f32[576,576]{0,1:T(8,128)}, f32[576,576]{0,1:T(8,128)S(1)}, u32[]{:S(2)}) copy-start(f32[576,576]{0,1:T(8,128)S(1)} %get-tuple-element.81) | copy-start | bytes 3981316
  203.2 7.9 %copy-start.42 = (bf16[576,1536]{0,1:T(8,128)(2,1)S(1)}, bf16[576,1536]{0,1:T(8,128)(2,1)}, u32[]{:S(2)}) copy-start(bf16[576,1536]{0,1:T(8,128)(2,1)} %all-gather.4.cloned.1.call-done) | copy-start | bytes 5308420
  211.1 1.7 copy-start.47
  211.1 1.8 copy-start.46
  211.1 2.8 copy-start.43
  213.9 1.9 copy-start.13
  215.8 1.8 copy-start.7
  217.7 2.2 copy-start.2
  219.7 128.1 %reduce-scatter.22.cloned.1.call-start = ((), (), s32[]{:S(2)}) async-start(), calls=%async_computation.13 | async-start | bytes 1658880
  229.4 0.9 copy-start.4
  229.4 1.3 copy-start.15
  230.7 3.1 copy-start.18
  230.7 3.1 copy-start.20
  237.9 3.5 copy-start.33
  237.9 3.5 copy-start.35
  244.7 190.3 %reduce-scatter.16.cloned.1.call-start = ((), (), s32[]{:S(2)}) async-start(), calls=%async_computation.10 | async-start | bytes 4423680 | tf_op jit(solution)/shard_map/reduce_scatter | solution.py:272
  250.3 272.5 %reduce-scatter.18.cloned.1.call-start = ((), (), s32[]{:S(2)}) async-start(), calls=%async_computation.11 | async-start | bytes 4423680 | tf_op jit(solution)/shard_map/reduce_scatter | solution.py:273
  256.0 349.6 %reduce-scatter.20.cloned.1.call-start = ((), (), s32[]{:S(2)}) async-start(), calls=%async_computation.12 | async-start | bytes 3981312 | tf_op jit(solution)/shard_map/reduce_scatter | solution.py:274
  261.3 407.9 %reduce-scatter.24.cloned.1.call-start = ((), (), s32[]{:S(2)}) async-start(), calls=%async_computation.14 | async-start | bytes 552960
  265.3 4.5 copy-start.1
  269.7 462.4 %reduce-scatter.26.cloned.1.call-start = ((), (), s32[]{:S(2)}) async-start(), calls=%async_computation.15 | async-start | bytes 552960
  271.9 1.9 copy-start.22
  271.9 1.9 copy-start.25
  272.5 3.0 copy-start.24
  275.4 1.7 copy-start.12
  277.0 22.1 %copy-start.3 = (f32[576,576]{0,1:T(8,128)S(1)}, f32[576,576]{0,1:T(8,128)}, u32[]{:S(2)}) copy-start(f32[576,576]{0,1:T(8,128)} %copy-done.2) | copy-start | bytes 3981316
  277.0 493.5 %all-reduce.14.cloned.1.call-start = ((), (), s32[]{:S(2)}) async-start(), calls=%async_computation.17 | async-start | bytes 1794048 | tf_op jit(solution)/shard_map/psum | solution.py:279
  349.4 257.9 %copy-start.6 = (f32[576,576]{0,1:T(8,128)S(1)}, f32[576,576]{0,1:T(8,128)}, u32[]{:S(2)}) copy-start(f32[576,576]{0,1:T(8,128)} %copy-done.5) | copy-start | bytes 3981316
  770.5 3.6 copy-start.27
  770.5 4.4 copy-start.31
  770.5 5.1 copy-start.30
Sparse Core Ops, SparseCore 0:
  10.2 52.3 all-gather.3
  64.8 52.4 all-gather.5
  119.4 51.4 all-gather.7
  219.8 61.4 reduce-scatter.27
  284.7 63.0 reduce-scatter.21
  351.3 83.5 reduce-scatter.15
  438.6 84.1 reduce-scatter.17
  526.4 79.0 reduce-scatter.19
  609.4 59.7 reduce-scatter.23
  673.0 59.0 reduce-scatter.25
  735.9 34.5 all-reduce.13
where the time goes:
time: 792 us; the launch traced here: 783 us
  waiting for transfers between devices  443 us (56%)
  blocking collectives  182 us (23%)
  matrix products  75.9 us (10%)
  local copies, waits for them, and re-layouts  33.9 us (4%)
  other arithmetic  31.8 us (4%)
  between operations  16.1 us (2%)
    unnamed x15, waiting for transfers between devices  165 us
    reduce_scatter x1, waiting for transfers between devices, body(): lax.psum_scatter(mlp_part[1], 'fsdp', scatter_dimension=1, tiled=True)  86.2 us
    reduce_scatter x1, waiting for transfers between devices, body(): lax.psum_scatter(mlp_part[0], 'fsdp', scatter_dimension=1, tiled=True)  85.5 us
    reduce_scatter x1, waiting for transfers between devices, body(): lax.psum_scatter(mlp_part[2], 'fsdp', scatter_dimension=1, tiled=True)  81 us
    dot_general x21, matrix products, matrix_product(): return jnp.dot(left, right, preferred_element_type=jnp.float32)  66.5 us
    unnamed x2, blocking collectives  41.7 us
    all_gather x1, blocking collectives, body(): lax.all_gather(w_query, 'fsdp', axis=1, tiled=True)  33.6 us
    all_gather x1, blocking collectives, body(): lax.all_gather(output_projection_weight, 'fsdp', axis=1, tiled=True)  32.6 us
  transfers between devices with their start and end apart: 11, of which 7 were waited for; matrix products, arithmetic and copies ran while one was open for 15% of the time, Pallas kernels for 0%

commit v1 on v0

--- a/solution.py
+++ b/solution.py
@@ -276,7 +276,7 @@
         lax.psum_scatter(mlp_part[3], "fsdp", scatter_dimension=0, tiled=True),
     )
     summed = (
-        lax.psum(shares[0].astype(jnp.bfloat16), "dp").astype(jnp.float32),
+        jnp.sum(lax.all_gather(shares[0].astype(jnp.bfloat16), "dp"), axis=0).astype(jnp.float32),
         lax.psum(shares[1].astype(jnp.bfloat16), "dp").astype(jnp.float32),
         lax.psum(shares[2].astype(jnp.bfloat16), "dp").astype(jnp.float32),
         lax.psum(shares[3].astype(jnp.bfloat16), "dp").astype(jnp.float32),

time: 792 us -> 806 us (1.018)
  waiting for transfers between devices: 443 us -> 454 us
    unnamed x107 -> x121, local copies, waits for them, and re-layouts: 13.1 us -> 16.7 us
  transfers between devices with their start and end apart: 11 -> 11, of which waited for: 7 -> 7; matrix products, arithmetic and copies ran while one was open for 15% -> 12% of each run, Pallas kernels for 0% -> 0%
where the time goes in v1:
time: 806 us; the launch traced here: 797 us
  waiting for transfers between devices  454 us (56%)
  blocking collectives  189 us (23%)
  matrix products  72.2 us (9%)
  local copies, waits for them, and re-layouts  35.9 us (4%)
  other arithmetic  28.7 us (4%)
  between operations  16.2 us (2%)
    unnamed x15, waiting for transfers between devices  172 us
    reduce_scatter x1, waiting for transfers between devices, body(): lax.psum_scatter(mlp_part[1], 'fsdp', scatter_dimension=1, tiled=True)  86.2 us
    reduce_scatter x1, waiting for transfers between devices, body(): lax.psum_scatter(mlp_part[0], 'fsdp', scatter_dimension=1, tiled=True)  85.8 us
    reduce_scatter x1, waiting for transfers between devices, body(): lax.psum_scatter(mlp_part[2], 'fsdp', scatter_dimension=1, tiled=True)  81 us
    dot_general x21, matrix products, matrix_product(): return jnp.dot(left, right, preferred_element_type=jnp.float32)  62.2 us
    unnamed x2, blocking collectives  41.5 us
    all_gather x1, blocking collectives, body(): lax.all_gather(w_query, 'fsdp', axis=1, tiled=True)  33.5 us
    all_gather x1, blocking collectives, body(): lax.all_gather(output_projection_weight, 'fsdp', axis=1, tiled=True)  33.1 us
  transfers between devices with their start and end apart: 11, of which 7 were waited for; matrix products, arithmetic and copies ran while one was open for 12% of the time, Pallas kernels for 0%

profile of v1, /device:TPU:0, one launch (start us, length us, event | category | flops | bytes accessed | tf_op | source)
XLA Modules:
  0.0 796.9 jit_solution(6345640401729448334)
XLA Ops:
  10.6 1.5 copy.76
  14.0 24.2 %all-reduce.9 = (bf16[576]{0:T(1024)(128)(2,1)S(1)}, bf16[576]{0:T(1024)(128)(2,1)}) all-reduce(bf16[576]{0:T(1024)(128)(2,1)S(1)} %dynamic-update-slice, bf16[576]{0:T(1024)(128)(2,1)S(1)} %dynamic-update-slice.1), channel_id=1, replica_groups=mesh['dp'=4,'fsdp'=8] {'fsdp'}, use_global_device_ids=true, to_apply=%add | all-reduce | flops 1152 | bytes 4608
  38.2 32.0 %all_gather.35 = bf16[576,192]{0,1:T(8,128)(2,1)S(1)} all-gather(bf16[576,24]{0,1:T(8,128)(2,1)S(1)} %copy-done.42), channel_id=1, replica_groups=mesh['dp'=4,'fsdp'=8] {'fsdp'}, dimensions={1}, use_global_device_ids=true | all-gather | bytes 248832 | tf_op jit(solution)/shard_map/all_gather | solution.py:254
  72.5 33.5 %all_gather.36 = bf16[576,576]{0,1:T(8,128)(2,1)S(1)} all-gather(bf16[576,72]{0,1:T(8,128)(2,1)S(1)} %copy-done.33), channel_id=1, replica_groups=mesh['dp'=4,'fsdp'=8] {'fsdp'}, dimensions={1}, use_global_device_ids=true | all-gather | bytes 746496 | tf_op jit(solution)/shard_map/all_gather | solution.py:253
  106.9 2.0 fusion.56
  109.0 2.8 reshape.146
  111.9 31.4 %all_gather.34 = bf16[576,192]{0,1:T(8,128)(2,1)S(1)} all-gather(bf16[576,24]{0,1:T(8,128)(2,1)S(1)} %copy-done.43), channel_id=1, replica_groups=mesh['dp'=4,'fsdp'=8] {'fsdp'}, dimensions={1}, use_global_device_ids=true | all-gather | bytes 248832 | tf_op jit(solution)/shard_map/all_gather | solution.py:255
  143.2 1.2 convolution_convert_fusion.2
  146.8 0.9 fusion.35
  147.7 2.8 fusion.3
  151.1 1.0 copy-done
  152.9 1.7 convert_element_type.235
  154.5 2.3 copy.88
  156.8 33.1 %all_gather.37 = bf16[576,576]{0,1:T(8,128)(2,1)S(1)} all-gather(bf16[576,72]{0,1:T(8,128)(2,1)S(1)} %copy-done.34), channel_id=1, replica_groups=mesh['dp'=4,'fsdp'=8] {'fsdp'}, dimensions={1}, use_global_device_ids=true | all-gather | bytes 746496 | tf_op jit(solution)/shard_map/all_gather | solution.py:256
  190.0 2.2 multiply_reduce_fusion.3
  192.2 1.2 multiply_convert_fusion.3
  193.4 5.2 fusion.61
  198.6 5.2 fusion.62
  203.8 7.8 multiply_convert_fusion
  211.6 1.7 fusion.63
  213.4 1.0 copy-done.50
  214.5 2.5 multiply_reduce_fusion.1
  217.4 1.2 copy-done.1
  219.4 2.5 reshape.174
  222.0 2.7 copy.91
  226.0 3.1 fusion.6
  229.1 1.0 convolution_bitcast_fusion.1
  230.3 1.0 copy.97
  231.3 2.0 convert_element_type.250
  233.3 2.2 fusion.49
  235.6 3.0 fusion.34
  238.6 1.0 copy.102
  239.6 2.0 convert_element_type.253
  241.6 2.2 fusion.47
  243.9 3.6 fusion.36
  247.5 5.5 fusion.66
  253.2 5.5 fusion.67
  258.8 5.0 fusion.68
  264.7 1.5 fusion.41
  267.0 1.5 fusion.31
  269.4 0.9 convert_element_type.249
  270.3 2.1 fusion.51
  275.1 2.4 fusion.26
  277.5 17.4 %all-reduce.8 = (bf16[576]{0:T(1024)(128)(2,1)S(1)}, bf16[576]{0:T(1024)(128)(2,1)S(1)}) all-reduce(f32[576]{0:T(1024)S(1)} %get-tuple-element.46, f32[576]{0:T(1024)S(1)} %copy-done.44), channel_id=10, replica_groups=mesh['dp'=4,'fsdp'=8] {'fsdp'}, use_global_device_ids=true, to_apply=%region_21.22.clone | all-reduce | flops 1152 | bytes 6912
  295.0 1.8 fusion.25
  296.8 1.2 copy.105
  298.4 3.6 add_convert_fusion
  302.0 1.2 copy.104
  304.0 51.5 %reduce-scatter.26.cloned.1.call-done = f32[576,24]{0,1:T(8,128)} async-done(((f32[576,192]{0,1:T(8,128)}), f32[576,24]{0,1:T(8,128)}) %reduce-scatter.26.cloned.1.call-update) | async-done | bytes 55312
  356.3 66.3 %reduce-scatter.28.cloned.1.call-done = f32[576,72]{0,1:T(8,128)} async-done(((f32[576,576]{0,1:T(8,128)}), f32[576,72]{0,1:T(8,128)}) %reduce-scatter.28.cloned.1.call-update) | async-done | bytes 165904
  422.6 1.6 convert_element_type.261
  424.1 85.8 %reduce-scatter.16.cloned.1.call-done = f32[576,192]{0,1:T(8,128)} async-done(((f32[576,1536]{0,1:T(8,128)}), f32[576,192]{0,1:T(8,128)}) %reduce-scatter.16.cloned.1.call-update) | async-done | bytes 442384 | tf_op jit(solution)/shard_map/reduce_scatter | solution.py:272
  509.9 1.8 convert_element_type.263
  511.7 86.2 %reduce-scatter.18.cloned.1.call-done = f32[576,192]{0,1:T(8,128)} async-done(((f32[576,1536]{0,1:T(8,128)}), f32[576,192]{0,1:T(8,128)}) %reduce-scatter.18.cloned.1.call-update) | async-done | bytes 442384 | tf_op jit(solution)/shard_map/reduce_scatter | solution.py:273
  597.9 1.8 convert_element_type.265
  599.7 81.0 %reduce-scatter.20.cloned.1.call-done = f32[1536,72]{0,1:T(8,128)} async-done(((f32[1536,576]{0,1:T(8,128)}), f32[1536,72]{0,1:T(8,128)}) %reduce-scatter.20.cloned.1.call-update) | async-done | bytes 442384 | tf_op jit(solution)/shard_map/reduce_scatter | solution.py:274
  680.7 1.7 convert_element_type.267
  682.4 11.1 %all-reduce.10 = (bf16[576,24]{0,1:T(8,128)(2,1)S(1)}, bf16[576,24]{0,1:T(8,128)(2,1)S(1)}, bf16[72]{0:T(256)(128)(2,1)S(1)}, bf16[72]{0:T(256)(128)(2,1)S(1)}) all-reduce(bf16[576,24]{0,1:T(8,128)(2,1)S(1)} %convert_element_type.257, bf16[576,24]{0,1:T(8,128)(2,1)S(1)} %convert_element_type.259, ...), channel_id=1, replica_groups=mesh['dp'=4,'fsdp'=8] {'dp'}, use_global_device_ids=true, to_apply=%region_9.10 | all-reduce | flops 27792 | bytes 111168 | tf_op jit(solution)/shard_map/psum | solution.py:280
  695.8 51.6 %reduce-scatter.22.cloned.1.call-done = f32[576,72]{0,1:T(8,128)} async-done(((f32[576,576]{0,1:T(8,128)}), f32[576,72]{0,1:T(8,128)}) %reduce-scatter.22.cloned.1.call-update) | async-done | bytes 165904
  747.4 0.9 convert_bitcast_fusion
  748.4 6.3 all-gather.1
  755.4 29.7 %all-reduce.14.cloned.1.call-done = (bf16[576,72]{0,1:T(8,128)(2,1)}, bf16[576,192]{0,1:T(8,128)(2,1)}, bf16[576,192]{0,1:T(8,128)(2,1)}, bf16[1536,72]{0,1:T(8,128)(2,1)}) async-done(((bf16[576,72]{0,1:T(8,128)(2,1)}, bf16[576,192]{0,1:T(8,128)(2,1)}, bf16[576,192]{0,1:T(8,128)(2,1)}, bf16[1536,72]{0,1:T(8,128)(2,1)}), (bf16[576,72]{0,1:T(8,128)(2,1)}, bf16[576,192]{0,1:T(8,128)(2,1)}, ...) | async-done | bytes 746512 | tf_op jit(solution)/shard_map/psum | solution.py:282
  785.1 1.8 convert_element_type.264
  786.9 1.8 convert_element_type.266
  (180 shorter events, 25.8 us)
Async XLA Ops:
  7.2 5.1 copy-start.46
  7.2 6.3 copy-start.51
  7.2 6.6 copy-start.52
  7.2 31.0 %copy-start.42 = (bf16[576,24]{0,1:T(8,128)(2,1)S(1)}, bf16[576,24]{0,1:T(8,128)(2,1)}, u32[]{:S(2)}) copy-start(bf16[576,24]{0,1:T(8,128)(2,1)} %param.14) | copy-start | bytes 82948
  7.2 186.2 %all-gather.6.cloned.1.call-start = ((), (), s32[]{:S(2)}) async-start(), calls=%async_computation.7 | async-start | bytes 2211840 | tf_op jit(solution)/shard_map/all_gather | solution.py:257
  8.0 190.6 %all-gather.8.cloned.1.call-start = ((), (), s32[]{:S(2)}) async-start(), calls=%async_computation.8 | async-start | bytes 2211840 | tf_op jit(solution)/shard_map/all_gather | solution.py:258
  8.7 195.1 %all-gather.10.cloned.1.call-start = ((), (), s32[]{:S(2)}) async-start(), calls=%async_computation.9 | async-start | bytes 1990656 | tf_op jit(solution)/shard_map/all_gather | solution.py:259
  9.4 293.7 %reduce-scatter.24.cloned.1.call-start = ((), (), s32[]{:S(2)}) async-start(), calls=%async_computation.14 | async-start | bytes 552960
  12.2 131.0 %copy-start.36 = (f32[576]{0:T(1024)}, f32[576]{0:T(1024)S(1)}, u32[]{:S(2)}) copy-start(f32[576]{0:T(1024)S(1)} %add_rsqrt_fusion.1) | copy-start | bytes 6916
  38.2 105.1 %copy-start.39 = (f32[576]{0:T(1024)}, f32[576]{0:T(1024)S(1)}, u32[]{:S(2)}) copy-start(f32[576]{0:T(1024)S(1)} %convert_element_type.226) | copy-start | bytes 6916
  71.3 1.2 copy-start.33
  106.1 0.9 copy-start.12
  109.0 2.9 copy-start.43
  111.8 32.5 %copy-start.47 = (f32[192]{0:T(256)S(1)}, f32[192]{0:T(256)}, u32[]{:S(2)}) copy-start(f32[192]{0:T(256)} %iota_convert_fusion) | copy-start | bytes 2308
  111.9 32.5 %copy-start.48 = (f32[32]{0:T(128)S(1)}, f32[32]{0:T(128)}, u32[]{:S(2)}) copy-start(f32[32]{0:T(128)} %negate_power_fusion) | copy-start | bytes 388
  143.2 1.4 copy-start.23
  144.6 85.5 %copy-start.27 = (f32[192,32]{0,1:T(8,128)}, f32[192,32]{0,1:T(8,128)S(1)}, u32[]{:S(2)}) copy-start(f32[192,32]{0,1:T(8,128)S(1)} %get-tuple-element.75) | copy-start | bytes 73732
  144.6 85.5 %copy-start.29 = (f32[192,32]{0,1:T(8,128)}, f32[192,32]{0,1:T(8,128)S(1)}, u32[]{:S(2)}) copy-start(f32[192,32]{0,1:T(8,128)S(1)} %get-tuple-element.76) | copy-start | bytes 73732
  144.6 1.0 copy-start.17
  145.6 0.9 copy-start.31
  145.8 1.9 copy-start.18
  145.8 1.9 copy-start.20
  145.9 1.8 copy-start.8
  146.6 1.1 copy-start.10
  146.8 3.8 copy-start.15
  150.5 1.6 copy-start
  152.9 1.7 copy-start.45
  152.9 4.0 copy-start.34
  190.0 2.2 copy-start.6
  192.2 24.8 %copy-start.4 = (f32[576,576]{0,1:T(8,128)}, f32[576,576]{0,1:T(8,128)S(1)}, u32[]{:S(2)}) copy-start(f32[576,576]{0,1:T(8,128)S(1)} %get-tuple-element.80) | copy-start | bytes 3981316
  203.8 7.8 copy-start.49
  211.6 1.7 copy-start.54
  211.6 1.8 copy-start.53
  211.6 2.8 copy-start.50
  214.5 2.5 copy-start.14
  217.0 1.6 copy-start.7
  217.4 1.2 copy-start.1
  224.7 0.9 copy-start.3
  224.7 1.3 copy-start.16
  226.0 3.1 copy-start.9
  226.0 3.1 copy-start.11
  230.1 3.2 copy-start.37
  230.1 3.2 copy-start.40
  235.5 119.9 %reduce-scatter.26.cloned.1.call-start = ((), (), s32[]{:S(2)}) async-start(), calls=%async_computation.15 | async-start | bytes 552960
  243.8 178.7 %reduce-scatter.28.cloned.1.call-start = ((), (), s32[]{:S(2)}) async-start(), calls=%async_computation.16 | async-start | bytes 1658880
  247.5 262.4 %reduce-scatter.16.cloned.1.call-start = ((), (), s32[]{:S(2)}) async-start(), calls=%async_computation.10 | async-start | bytes 4423680 | tf_op jit(solution)/shard_map/reduce_scatter | solution.py:272
  253.1 344.8 %reduce-scatter.18.cloned.1.call-start = ((), (), s32[]{:S(2)}) async-start(), calls=%async_computation.11 | async-start | bytes 4423680 | tf_op jit(solution)/shard_map/reduce_scatter | solution.py:273
  258.7 421.9 %reduce-scatter.20.cloned.1.call-start = ((), (), s32[]{:S(2)}) async-start(), calls=%async_computation.12 | async-start | bytes 3981312 | tf_op jit(solution)/shard_map/reduce_scatter | solution.py:274
  263.8 0.9 copy-start.19
  263.9 483.6 %reduce-scatter.22.cloned.1.call-start = ((), (), s32[]{:S(2)}) async-start(), calls=%async_computation.13 | async-start | bytes 1658880
  266.2 0.8 copy-start.30
  269.4 1.0 copy-start.38
  269.4 1.0 copy-start.41
  272.4 0.9 copy-start.22
  272.4 1.1 copy-start.25
  272.4 1.5 copy-start.24
  272.4 1.5 copy-start.26
  272.4 512.7 %all-reduce.14.cloned.1.call-start = ((), (), s32[]{:S(2)}) async-start(), calls=%async_computation.17 | async-start | bytes 1609728 | tf_op jit(solution)/shard_map/psum | solution.py:282
  274.0 1.1 copy-start.13
  275.1 2.4 copy-start.44
  275.1 19.9 %copy-start.2 = (f32[576,576]{0,1:T(8,128)S(1)}, f32[576,576]{0,1:T(8,128)}, u32[]{:S(2)}) copy-start(f32[576,576]{0,1:T(8,128)} %copy-done.1) | copy-start | bytes 3981316
  296.8 1.6 copy-start.5
  785.1 3.6 copy-start.32
  785.1 4.4 copy-start.35
  (2 other events, 1.5 us)
Sparse Core Ops, SparseCore 0:
  10.2 52.4 all-gather.5
  64.9 53.3 all-gather.7
  120.5 50.8 all-gather.9
  235.7 57.1 reduce-scatter.23
  296.6 58.8 reduce-scatter.25
  358.8 63.6 reduce-scatter.27
  426.3 83.6 reduce-scatter.15
  513.6 84.2 reduce-scatter.17
  601.6 79.0 reduce-scatter.19
  684.0 63.3 reduce-scatter.21
  751.2 33.8 all-reduce.13
